TPU v7x, 32 devices: a whole 2x2x4 slice. The times are simulated.
32 devices in a mesh: fsdp: 2 (over x), context: 4 (over y, core), tensor: 4 (over z).
Axes of the slice: x: 2, y: 2, z: 4, core: 2. Of those that a mesh axis runs over, the one named last changes fastest.
Arguments:
- hidden_in: bfloat16 [2, 1024, 2048], P('fsdp', ('context', 'tensor')), may hold values from -6 to 6
- segment_ids: int32 [2, 1024], P('fsdp'), may hold values from 0 to 15, never falling along the last dimension, each value on 1 to 512 neighbouring positions
- pad_mask: int32 [2, 1024], P('fsdp'), may hold values from 0 to 1, as said below
- attn_gain: bfloat16 [2048], P(('fsdp', 'context')), may hold values from 0.5 to 1.5
- w_query: bfloat16 [2048, 2048], P(('fsdp', 'context'), 'tensor'), may hold values from -0.1875 to 0.1875
- w_key: bfloat16 [2048, 256], P(('fsdp', 'context'), 'tensor'), may hold values from -0.1875 to 0.1875
- w_value: bfloat16 [2048, 256], P(('fsdp', 'context'), 'tensor'), may hold values from -0.125 to 0.125
- w_out: bfloat16 [2048, 2048], P('tensor', ('fsdp', 'context')), may hold values from -0.5 to 0.5
- mlp_gain: bfloat16 [2048], P(('fsdp', 'context')), may hold values from 0.5 to 1.5
- w_gate: bfloat16 [2048, 5632], P(('fsdp', 'context'), 'tensor'), may hold values from -0.125 to 0.125
- w_up: bfloat16 [2048, 5632], P(('fsdp', 'context'), 'tensor'), may hold values from -0.125 to 0.125
- w_down: bfloat16 [5632, 2048], P('tensor', ('fsdp', 'context')), may hold values from -0.078125 to 0.078125
- cotangent: bfloat16 [2, 1024, 2048], P('fsdp', ('context', 'tensor')), may hold values from -6 to 6
Outputs:
- block_out: bfloat16 [2, 1024, 2048], P('fsdp', ('context', 'tensor'))
- grad_hidden: float32 [2, 1024, 2048], P('fsdp', ('context', 'tensor'))
- grad_attn_gain: float32 [2048], P(('fsdp', 'context'))
- grad_query: float32 [2048, 2048], P(('fsdp', 'context'), 'tensor')
- grad_key: float32 [2048, 256], P(('fsdp', 'context'), 'tensor')
- grad_value: float32 [2048, 256], P(('fsdp', 'context'), 'tensor')
- grad_out: float32 [2048, 2048], P('tensor', ('fsdp', 'context'))
- grad_mlp_gain: float32 [2048], P(('fsdp', 'context'))
- grad_gate: float32 [2048, 5632], P(('fsdp', 'context'), 'tensor')
- grad_up: float32 [2048, 5632], P(('fsdp', 'context'), 'tensor')
- grad_down: float32 [5632, 2048], P('tensor', ('fsdp', 'context'))
Inputs may be any that keep to these rules, and one draw needn't show every extreme that they name: `segment_ids`: ids never fall along a sequence; a document is a run of 1 to 512 consecutive tokens of one id. `pad_mask`: every sequence ends in one or more padding slots, and no other slot is padding.
All inputs are finite; a program needn't handle non-finite values.
Results may differ from a plain program's by a relative error of at most 0.013.
The roundings to bfloat16 on the way count: a program that leaves them out, or rounds other values in their place, can miss the bound.
Values may be sent and summed in bfloat16 or wider, within the bound.
A program may use at most 88 MiB of HBM per device.

v0:
```python
import math
import jax
import jax.numpy as jnp
from jax import lax
from jax.sharding import PartitionSpec as P

EPS = 1e-05
NEG = -1e30


def positions_of(segments):
    length = segments.shape[1]
    columns = jnp.arange(length, dtype=jnp.int32)[None, :]
    previous = jnp.concatenate(
        [jnp.full((segments.shape[0], 1), -1, jnp.int32), segments[:, :-1]], axis=1
    )
    starts = jnp.where(segments != previous, columns, jnp.zeros_like(columns))
    return columns - lax.cummax(starts, axis=1)


def rope_tables(positions, head_size):
    half_size = head_size // 2
    frequency = jnp.exp(
        -(jnp.arange(half_size, dtype=jnp.float32) * (2.0 / head_size)) * math.log(10000.0)
    )
    angles = positions.astype(jnp.float32)[..., None] * frequency
    return (jnp.cos(angles)[..., None, :], jnp.sin(angles)[..., None, :])


def rotate(vectors, cos_table, sin_table):
    half_size = vectors.shape[-1] // 2
    first_half = vectors[..., :half_size]
    second_half = vectors[..., half_size:]
    return jnp.concatenate(
        [
            first_half * cos_table - second_half * sin_table,
            second_half * cos_table + first_half * sin_table,
        ],
        axis=-1,
    )


def allowed_of(seg_row, pad_row):
    length = seg_row.shape[0]
    columns = jnp.arange(length, dtype=jnp.int32)
    same_doc = seg_row[:, None] == seg_row[None, :]
    causal = columns[None, :] <= columns[:, None]
    live_key = (pad_row[None, :] == 1) | (columns[:, None] == columns[None, :])
    return same_doc & causal & live_key


def matmul(left_side, right_side):
    return jnp.dot(left_side, right_side, preferred_element_type=jnp.float32)


def matmul_left_t(left_side, right_side):
    return lax.dot_general(
        left_side, right_side, (((0,), (0,)), ((), ())), preferred_element_type=jnp.float32
    )


def matmul_right_t(left_side, right_side):
    return lax.dot_general(
        left_side, right_side, (((1,), (1,)), ((), ())), preferred_element_type=jnp.float32
    )


def rows_gather(activations):
    return lax.all_gather(activations, "tensor", axis=1, tiled=True)


def rows_sum(partials):
    return lax.psum_scatter(partials, "tensor", scatter_dimension=1, tiled=True)


def to_heads(by_rows):
    return lax.all_to_all(by_rows, "context", split_axis=2, concat_axis=1, tiled=True)


def to_spans(by_heads):
    return lax.all_to_all(by_heads, "context", split_axis=1, concat_axis=2, tiled=True)


def norm_back(grad_normed, vectors, inv_scale, gain_row):
    unit_rows = vectors * inv_scale
    weighted = grad_normed * gain_row.astype(jnp.float32)
    grad_gain = jnp.sum(grad_normed * unit_rows, axis=(0, 1))
    grad_vectors = inv_scale * (
        weighted - unit_rows * jnp.mean(weighted * unit_rows, axis=-1, keepdims=True)
    )
    return (grad_vectors, grad_gain)


def attend_scores(query_rows, kv_rows, seg_row, pad_row):
    length = query_rows.shape[0]
    head_size = kv_rows.shape[1] // 2
    query_heads = query_rows.reshape(length, -1, head_size)
    key_rows = kv_rows[:, :head_size]
    value_rows = kv_rows[:, head_size:]
    scores = jnp.einsum(
        "qhd,td->hqt", query_heads, key_rows, preferred_element_type=jnp.float32
    ) * head_size ** (-0.5)
    scores = jnp.where(allowed_of(seg_row, pad_row)[None], scores, NEG)
    return (query_heads, key_rows, value_rows, scores)


def attend_forward(packed_item):
    query_rows, kv_rows, seg_row, pad_row = packed_item
    query_heads, key_rows, value_rows, scores = attend_scores(query_rows, kv_rows, seg_row, pad_row)
    row_max = jnp.max(scores, axis=-1, keepdims=True)
    exp_scores = jnp.exp(scores - row_max)
    row_total = jnp.sum(exp_scores, axis=-1, keepdims=True)
    weights = exp_scores / row_total
    output = jnp.einsum(
        "hqt,td->qhd", weights.astype(jnp.bfloat16), value_rows, preferred_element_type=jnp.float32
    )
    output = output.reshape(query_rows.shape[0], -1).astype(jnp.bfloat16)
    return (output, (row_max + jnp.log(row_total))[..., 0])


def attend_backward(packed_item):
    query_rows, kv_rows, grad_rows, log_total, seg_row, pad_row = packed_item
    query_heads, key_rows, value_rows, scores = attend_scores(query_rows, kv_rows, seg_row, pad_row)
    head_size = key_rows.shape[1]
    scale = head_size ** (-0.5)
    weights = jnp.exp(scores - log_total[..., None])
    grad_heads = grad_rows.reshape(query_heads.shape)
    grad_weights = jnp.einsum(
        "qhd,td->hqt", grad_heads, value_rows, preferred_element_type=jnp.float32
    )
    row_delta = jnp.sum(weights * grad_weights, axis=-1, keepdims=True)
    grad_scores = (weights * (grad_weights - row_delta)).astype(jnp.bfloat16)
    grad_queries = (
        jnp.einsum("hqt,td->qhd", grad_scores, key_rows, preferred_element_type=jnp.float32) * scale
    )
    grad_keys = (
        jnp.einsum("hqt,qhd->td", grad_scores, query_heads, preferred_element_type=jnp.float32)
        * scale
    )
    grad_values = jnp.einsum(
        "hqt,qhd->td", weights.astype(jnp.bfloat16), grad_heads, preferred_element_type=jnp.float32
    )
    return (grad_queries, jnp.concatenate([grad_keys, grad_values], axis=-1))


def forward_pass(params, tables):
    hidden_in, attn_gain, w_query, w_key, w_value, w_out, mlp_gain, w_gate, w_up, w_down = params
    cos_span, sin_span, segment_ids, pad_mask, keep_rows = tables
    gain_one, query_all, key_all, value_all, out_all = (
        lax.all_gather(attn_gain, ("fsdp", "context"), axis=0, tiled=True),
        lax.all_gather(w_query, ("fsdp", "context"), axis=0, tiled=True),
        lax.all_gather(w_key, ("fsdp", "context"), axis=0, tiled=True),
        lax.all_gather(w_value, ("fsdp", "context"), axis=0, tiled=True),
        lax.all_gather(w_out, ("fsdp", "context"), axis=1, tiled=True),
    )
    seq_count, row_count, model_width = hidden_in.shape
    head_size = key_all.shape[1]
    hidden_f = hidden_in.astype(jnp.float32)
    scale_one = lax.rsqrt(jnp.mean(hidden_f * hidden_f, axis=-1, keepdims=True) + EPS)
    normed_one = rows_gather(
        (hidden_f * scale_one * gain_one.astype(jnp.float32)).astype(jnp.bfloat16)
    )
    span_len = normed_one.shape[1]
    flat_one = normed_one.reshape(-1, model_width)
    query_pre = matmul(flat_one, query_all).reshape(seq_count, span_len, -1, head_size)
    queries = (
        rotate(query_pre, cos_span, sin_span).astype(jnp.bfloat16).reshape(seq_count, span_len, -1)
    )
    key_pre = matmul(flat_one, key_all).reshape(seq_count, span_len, 1, head_size)
    key_rows = (
        rotate(key_pre, cos_span, sin_span)
        .astype(jnp.bfloat16)
        .reshape(seq_count, span_len, head_size)
    )
    value_rows = (
        matmul(flat_one, value_all).astype(jnp.bfloat16).reshape(seq_count, span_len, head_size)
    )
    query_full = to_heads(queries)
    kv_full = lax.all_gather(
        jnp.concatenate([key_rows, value_rows], axis=-1), "context", axis=1, tiled=True
    )
    attn_full, log_total = lax.map(attend_forward, (query_full, kv_full, segment_ids, pad_mask))
    out_span = to_spans(attn_full)
    out_flat = out_span.reshape(-1, out_span.shape[2])
    branch_one = rows_sum(matmul(out_flat, out_all).reshape(seq_count, span_len, model_width))
    middle = hidden_f + branch_one
    gain_two, gate_all, up_all, down_all = (
        lax.all_gather(mlp_gain, ("fsdp", "context"), axis=0, tiled=True),
        lax.all_gather(w_gate, ("fsdp", "context"), axis=0, tiled=True),
        lax.all_gather(w_up, ("fsdp", "context"), axis=0, tiled=True),
        lax.all_gather(w_down, ("fsdp", "context"), axis=1, tiled=True),
    )
    scale_two = lax.rsqrt(jnp.mean(middle * middle, axis=-1, keepdims=True) + EPS)
    normed_two = rows_gather(
        (middle * scale_two * gain_two.astype(jnp.float32)).astype(jnp.bfloat16)
    )
    flat_two = normed_two.reshape(-1, model_width)
    gate_rows = matmul(flat_two, gate_all)
    up_rows = matmul(flat_two, up_all)
    inner_rows = (jax.nn.silu(gate_rows) * up_rows).astype(jnp.bfloat16)
    branch_two = rows_sum(matmul(inner_rows, down_all).reshape(seq_count, span_len, model_width))
    block_out = (keep_rows * (middle + branch_two)).astype(jnp.bfloat16)
    return dict(
        block_out=block_out,
        gain_one=gain_one,
        query_all=query_all,
        key_all=key_all,
        value_all=value_all,
        out_all=out_all,
        gain_two=gain_two,
        gate_all=gate_all,
        up_all=up_all,
        down_all=down_all,
        hidden_f=hidden_f,
        scale_one=scale_one,
        flat_one=flat_one,
        query_full=query_full,
        kv_full=kv_full,
        log_total=log_total,
        out_flat=out_flat,
        middle=middle,
        scale_two=scale_two,
        flat_two=flat_two,
        gate_rows=gate_rows,
        up_rows=up_rows,
        inner_rows=inner_rows,
    )


def body(
    hidden_in,
    segment_ids,
    pad_mask,
    attn_gain,
    w_query,
    w_key,
    w_value,
    w_out,
    mlp_gain,
    w_gate,
    w_up,
    w_down,
    cotangent,
):
    seq_count, row_count, model_width = hidden_in.shape
    context_count = lax.axis_size("context")
    tensor_count = lax.axis_size("tensor")
    context_index = lax.axis_index("context")
    tensor_index = lax.axis_index("tensor")
    seq_length = segment_ids.shape[1]
    span_len = seq_length // context_count
    head_size = w_key.shape[1]
    cos_full, sin_full = rope_tables(positions_of(segment_ids), head_size)
    cos_span = lax.dynamic_slice_in_dim(cos_full, context_index * span_len, span_len, 1)
    sin_span = lax.dynamic_slice_in_dim(sin_full, context_index * span_len, span_len, 1)
    row_start = (context_index * tensor_count + tensor_index) * row_count
    keep_rows = lax.dynamic_slice_in_dim(pad_mask, row_start, row_count, 1).astype(jnp.float32)[
        ..., None
    ]
    tables = (cos_span, sin_span, segment_ids, pad_mask, keep_rows)
    params = (hidden_in, attn_gain, w_query, w_key, w_value, w_out, mlp_gain, w_gate, w_up, w_down)
    first_pass = forward_pass(params, tables)
    saved_state = forward_pass(lax.optimization_barrier(params), tables)
    grad_rows = cotangent.astype(jnp.float32) * keep_rows
    grad_down_in = rows_gather(grad_rows.astype(jnp.bfloat16)).reshape(-1, model_width)
    grad_down = matmul_left_t(saved_state["inner_rows"], grad_down_in)
    grad_inner = matmul_right_t(grad_down_in, saved_state["down_all"])
    gate_rows = saved_state["gate_rows"]
    sigmoid_gate = jax.nn.sigmoid(gate_rows)
    grad_gate_rows = (
        grad_inner
        * saved_state["up_rows"]
        * sigmoid_gate
        * (1.0 + gate_rows * (1.0 - sigmoid_gate))
    ).astype(jnp.bfloat16)
    grad_up_rows = (grad_inner * gate_rows * sigmoid_gate).astype(jnp.bfloat16)
    grad_gate = matmul_left_t(saved_state["flat_two"], grad_gate_rows)
    grad_up = matmul_left_t(saved_state["flat_two"], grad_up_rows)
    grad_gate, grad_up, grad_down = (
        lax.psum_scatter(grad_gate, ("fsdp", "context"), scatter_dimension=0, tiled=True),
        lax.psum_scatter(grad_up, ("fsdp", "context"), scatter_dimension=0, tiled=True),
        lax.psum_scatter(grad_down, ("fsdp", "context"), scatter_dimension=1, tiled=True),
    )
    grad_normed_two = matmul_right_t(grad_gate_rows, saved_state["gate_all"]) + matmul_right_t(
        grad_up_rows, saved_state["up_all"]
    )
    grad_normed_two = rows_sum(grad_normed_two.reshape(seq_count, span_len, model_width))
    grad_middle_norm, grad_gain_two = norm_back(
        grad_normed_two, saved_state["middle"], saved_state["scale_two"], saved_state["gain_two"]
    )
    grad_middle = grad_rows + grad_middle_norm
    grad_attn_in = rows_gather(grad_middle.astype(jnp.bfloat16)).reshape(-1, model_width)
    grad_out = matmul_left_t(saved_state["out_flat"], grad_attn_in)
    grad_attn_rows = matmul_right_t(grad_attn_in, saved_state["out_all"]).astype(jnp.bfloat16)
    grad_heads = to_heads(grad_attn_rows.reshape(seq_count, span_len, -1))
    grad_query_full, grad_kv_full = lax.map(
        attend_backward,
        (
            saved_state["query_full"],
            saved_state["kv_full"],
            grad_heads,
            saved_state["log_total"],
            segment_ids,
            pad_mask,
        ),
    )
    grad_query_full = (
        rotate(grad_query_full, cos_full, -sin_full)
        .astype(jnp.bfloat16)
        .reshape(seq_count, seq_length, -1)
    )
    grad_query_rows = to_spans(grad_query_full).reshape(seq_count * span_len, -1)
    grad_kv_span = lax.psum_scatter(grad_kv_full, "context", scatter_dimension=1, tiled=True)
    grad_key_rows = rotate(
        grad_kv_span[..., :head_size].reshape(seq_count, span_len, 1, head_size),
        cos_span,
        -sin_span,
    )
    grad_key_rows = grad_key_rows.astype(jnp.bfloat16).reshape(-1, head_size)
    grad_value_rows = grad_kv_span[..., head_size:].astype(jnp.bfloat16).reshape(-1, head_size)
    flat_one = saved_state["flat_one"]
    grad_query = matmul_left_t(flat_one, grad_query_rows)
    grad_key = matmul_left_t(flat_one, grad_key_rows)
    grad_value = matmul_left_t(flat_one, grad_value_rows)
    grad_normed_one = (
        matmul_right_t(grad_query_rows, saved_state["query_all"])
        + matmul_right_t(grad_key_rows, saved_state["key_all"])
        + matmul_right_t(grad_value_rows, saved_state["value_all"])
    )
    grad_normed_one = rows_sum(grad_normed_one.reshape(seq_count, span_len, model_width))
    grad_input_norm, grad_gain_one = norm_back(
        grad_normed_one, saved_state["hidden_f"], saved_state["scale_one"], saved_state["gain_one"]
    )
    grad_hidden = grad_middle + grad_input_norm
    grad_gain_one, grad_gain_two = lax.psum((grad_gain_one, grad_gain_two), "tensor")
    grad_gain_one, grad_query, grad_key, grad_value, grad_out, grad_gain_two = (
        lax.psum_scatter(grad_gain_one, ("fsdp", "context"), scatter_dimension=0, tiled=True),
        lax.psum_scatter(grad_query, ("fsdp", "context"), scatter_dimension=0, tiled=True),
        lax.psum_scatter(grad_key, ("fsdp", "context"), scatter_dimension=0, tiled=True),
        lax.psum_scatter(grad_value, ("fsdp", "context"), scatter_dimension=0, tiled=True),
        lax.psum_scatter(grad_out, ("fsdp", "context"), scatter_dimension=1, tiled=True),
        lax.psum_scatter(grad_gain_two, ("fsdp", "context"), scatter_dimension=0, tiled=True),
    )
    return (
        first_pass["block_out"],
        grad_hidden,
        grad_gain_one,
        grad_query,
        grad_key,
        grad_value,
        grad_out,
        grad_gain_two,
        grad_gate,
        grad_up,
        grad_down,
    )


def solution(mesh):
    in_specs = (
        P("fsdp", ("context", "tensor"), None),
        P("fsdp", None),
        P("fsdp", None),
        P(("fsdp", "context")),
        P(("fsdp", "context"), "tensor"),
        P(("fsdp", "context"), "tensor"),
        P(("fsdp", "context"), "tensor"),
        P("tensor", ("fsdp", "context")),
        P(("fsdp", "context")),
        P(("fsdp", "context"), "tensor"),
        P(("fsdp", "context"), "tensor"),
        P("tensor", ("fsdp", "context")),
        P("fsdp", ("context", "tensor"), None),
    )
    out_specs = (
        P("fsdp", ("context", "tensor"), None),
        P("fsdp", ("context", "tensor"), None),
        P(("fsdp", "context")),
        P(("fsdp", "context"), "tensor"),
        P(("fsdp", "context"), "tensor"),
        P(("fsdp", "context"), "tensor"),
        P("tensor", ("fsdp", "context")),
        P(("fsdp", "context")),
        P(("fsdp", "context"), "tensor"),
        P(("fsdp", "context"), "tensor"),
        P("tensor", ("fsdp", "context")),
    )
    return jax.shard_map(body, mesh=mesh, in_specs=in_specs, out_specs=out_specs, check_vma=False)
```

profile of v0, /device:TPU:0, one launch (start us, length us, event | category | flops | bytes accessed | tf_op | source)
XLA Modules:
  0.0 1386.3 jit_solution(9212681209821931771)
XLA Ops:
  9.0 10.3 all-gather.2
  23.4 8.8 all-gather
  37.4 9.1 all_gather.92
  46.5 9.6 all_gather.93
  65.9 13.0 all-gather.37.cloned.1.call-done
  82.9 25.8 %all-gather.23.cloned.1.call-done = bf16[2048,512]{1,0:T(8,128)(2,1)} async-done(((bf16[256,512]{1,0:T(8,128)(2,1)}), bf16[2048,512]{1,0:T(8,128)(2,1)}) %all-gather.23.cloned.1.call-update) | async-done | bytes 2097168 | tf_op jit(solution)/shard_map/all_gather | solution.py:151
  114.8 23.8 %all-gather.21.cloned.1.call-done = bf16[1,256,2048]{2,1,0:T(8,128)(2,1)} async-done(((bf16[1,64,2048]{2,1,0:T(8,128)(2,1)}), bf16[1,256,2048]{2,1,0:T(8,128)(2,1)}) %all-gather.21.cloned.1.call-update) | async-done | bytes 1048592 | tf_op jit(solution)/shard_map/all_gather | solution.py:69
  148.4 9.6 all_gather.94
  169.3 8.4 all_to_all.90
  182.1 8.8 all-gather.3
  191.0 35.0 %reduce-scatter.18.cloned.1.call-done = f32[1,64,2048]{2,1,0:T(8,128)} async-done(((f32[1,256,2048]{2,1,0:T(8,128)}), f32[1,64,2048]{2,1,0:T(8,128)}) %reduce-scatter.18.cloned.1.call-update) | async-done | bytes 524304 | tf_op jit(solution)/shard_map/reduce_scatter | solution.py:73
  233.9 22.6 %all-gather.45.cloned.1.call-done = bf16[1,256,2048]{2,1,0:T(8,128)(2,1)} async-done(((bf16[1,64,2048]{2,1,0:T(8,128)(2,1)}), bf16[1,256,2048]{2,1,0:T(8,128)(2,1)}) %all-gather.45.cloned.1.call-update) | async-done | bytes 1048592 | tf_op jit(solution)/shard_map/all_gather | solution.py:69
  256.5 44.9 %all-gather.47.cloned.1.call-done = bf16[2048,1408]{1,0:T(8,128)(2,1)} async-done(((bf16[256,1408]{1,0:T(8,128)(2,1)}), bf16[2048,1408]{1,0:T(8,128)(2,1)}) %all-gather.47.cloned.1.call-update) | async-done | bytes 5767184 | tf_op jit(solution)/shard_map/all_gather | solution.py:190
  301.4 5.9 fusion.40
  307.3 39.5 %all-gather.49.cloned.1.call-done = bf16[2048,1408]{1,0:T(8,128)(2,1)} async-done(((bf16[256,1408]{1,0:T(8,128)(2,1)}), bf16[2048,1408]{1,0:T(8,128)(2,1)}) %all-gather.49.cloned.1.call-update) | async-done | bytes 5767184 | tf_op jit(solution)/shard_map/all_gather | solution.py:189
  352.3 24.5 %all-gather.41.cloned.1.call-done = bf16[1,256,2048]{2,1,0:T(8,128)(2,1)} async-done(((bf16[1,64,2048]{2,1,0:T(8,128)(2,1)}), bf16[1,256,2048]{2,1,0:T(8,128)(2,1)}) %all-gather.41.cloned.1.call-update) | async-done | bytes 1048592 | tf_op jit(solution)/shard_map/all_gather | solution.py:69
  376.8 45.9 %all-gather.43.cloned.1.call-done = bf16[1408,2048]{1,0:T(8,128)(2,1)} async-done(((bf16[1408,256]{1,0:T(8,128)(2,1)}), bf16[1408,2048]{1,0:T(8,128)(2,1)}) %all-gather.43.cloned.1.call-update) | async-done | bytes 5767184 | tf_op jit(solution)/shard_map/all_gather | solution.py:191
  422.7 6.1 multiply_convert_fusion.1
  436.7 44.0 %reduce-scatter.20.cloned.1.call-done = f32[1,64,2048]{2,1,0:T(8,128)} async-done(((f32[1,256,2048]{2,1,0:T(8,128)}), f32[1,64,2048]{2,1,0:T(8,128)}) %reduce-scatter.20.cloned.1.call-update) | async-done | bytes 524304 | tf_op jit(solution)/shard_map/reduce_scatter | solution.py:73
  484.6 27.4 %all-gather.51.cloned.1.call-done = bf16[1,256,2048]{2,1,0:T(8,128)(2,1)} async-done(((bf16[1,64,2048]{2,1,0:T(8,128)(2,1)}), bf16[1,256,2048]{2,1,0:T(8,128)(2,1)}) %all-gather.51.cloned.1.call-update) | async-done | bytes 1048592 | tf_op jit(solution)/shard_map/all_gather | solution.py:69
  547.6 10.8 all_gather.80
  558.4 10.7 all_gather.81
  578.8 5.9 all-to-all-done
  587.1 7.3 all_gather.82
  594.4 6.5 fusion.117
  607.8 8.4 all_to_all.91
  621.1 9.3 all-gather.1
  630.5 33.1 %reduce-scatter.14.cloned.1.call-done = f32[1,64,2048]{2,1,0:T(8,128)} async-done(((f32[1,256,2048]{2,1,0:T(8,128)}), f32[1,64,2048]{2,1,0:T(8,128)}) %reduce-scatter.14.cloned.1.call-update) | async-done | bytes 524304 | tf_op jit(solution)/shard_map/reduce_scatter | solution.py:73
  680.1 10.2 all_to_all.92
  700.8 7.2 all-gather.29.cloned.1.call-done
  708.0 30.0 %all-gather.27.cloned.1.call-done = bf16[1,256,2048]{2,1,0:T(8,128)(2,1)} async-done(((bf16[1,64,2048]{2,1,0:T(8,128)(2,1)}), bf16[1,256,2048]{2,1,0:T(8,128)(2,1)}) %all-gather.27.cloned.1.call-update) | async-done | bytes 1048592 | tf_op jit(solution)/shard_map/all_gather | solution.py:69
  738.0 5.9 fusion.56
  743.9 38.8 %all-gather.31.cloned.1.call-done = bf16[2048,1408]{1,0:T(8,128)(2,1)} async-done(((bf16[256,1408]{1,0:T(8,128)(2,1)}), bf16[2048,1408]{1,0:T(8,128)(2,1)}) %all-gather.31.cloned.1.call-update) | async-done | bytes 5767184 | tf_op jit(solution)/shard_map/all_gather | solution.py:190
  782.7 46.1 %all-gather.33.cloned.1.call-done = bf16[1408,2048]{1,0:T(8,128)(2,1)} async-done(((bf16[1408,256]{1,0:T(8,128)(2,1)}), bf16[1408,2048]{1,0:T(8,128)(2,1)}) %all-gather.33.cloned.1.call-update) | async-done | bytes 5767184 | tf_op jit(solution)/shard_map/all_gather | solution.py:191
  828.8 9.5 convolution_bitcast_fusion.1
  847.7 6.1 fusion.36
  854.9 6.1 fusion.34
  862.6 7.3 fusion.42
  876.3 24.0 %all-reduce.2 = (f32[2048]{0:T(1024)S(1)}, f32[2048]{0:T(1024)S(1)}) all-reduce(f32[2048]{0:T(1024)S(1)} %get-tuple-element.99, f32[2048]{0:T(1024)S(1)} %copy-done.37), channel_id=8, replica_groups=mesh['fsdp'=2,'context'=4,'tensor'=4] {'fsdp','context'}, use_global_device_ids=true, to_apply=%region_21.22.clone | all-reduce | flops 4096 | bytes 32768
  900.5 11.3 all-reduce.3
  913.9 6.9 reduce-scatter.16.cloned.1.call-done
  922.7 35.3 %reduce-scatter.28.cloned.1.call-done = f32[256,64]{0,1:T(8,128)} async-done(((f32[2048,64]{0,1:T(8,128)}), f32[256,64]{0,1:T(8,128)}) %reduce-scatter.28.cloned.1.call-update) | async-done | bytes 65552 | tf_op jit(solution)/shard_map/reduce_scatter | solution.py:339
  958.0 38.0 %reduce-scatter.30.cloned.1.call-done = f32[256,64]{0,1:T(8,128)} async-done(((f32[2048,64]{0,1:T(8,128)}), f32[256,64]{0,1:T(8,128)}) %reduce-scatter.30.cloned.1.call-update) | async-done | bytes 65552 | tf_op jit(solution)/shard_map/reduce_scatter | solution.py:340
  996.0 55.3 %reduce-scatter.32.cloned.1.call-done = f32[512,256]{1,0:T(8,128)} async-done(((f32[512,2048]{1,0:T(8,128)}), f32[512,256]{1,0:T(8,128)}) %reduce-scatter.32.cloned.1.call-update) | async-done | bytes 524304 | tf_op jit(solution)/shard_map/reduce_scatter | solution.py:341
  1051.3 55.5 %reduce-scatter.26.cloned.1.call-done = f32[256,512]{1,0:T(8,128)} async-done(((f32[2048,512]{1,0:T(8,128)}), f32[256,512]{1,0:T(8,128)}) %reduce-scatter.26.cloned.1.call-update) | async-done | bytes 524304 | tf_op jit(solution)/shard_map/reduce_scatter | solution.py:338
  1106.8 90.7 %reduce-scatter.34.cloned.1.call-done = f32[256,1408]{1,0:T(8,128)} async-done(((f32[2048,1408]{1,0:T(8,128)}), f32[256,1408]{1,0:T(8,128)}) %reduce-scatter.34.cloned.1.call-update) | async-done | bytes 1441808 | tf_op jit(solution)/shard_map/reduce_scatter | solution.py:280
  1197.5 90.9 %reduce-scatter.36.cloned.1.call-done = f32[256,1408]{1,0:T(8,128)} async-done(((f32[2048,1408]{1,0:T(8,128)}), f32[256,1408]{1,0:T(8,128)}) %reduce-scatter.36.cloned.1.call-update) | async-done | bytes 1441808 | tf_op jit(solution)/shard_map/reduce_scatter | solution.py:281
  1288.4 90.9 %reduce-scatter.38.cloned.1.call-done = f32[1408,256]{1,0:T(8,128)} async-done(((f32[1408,2048]{1,0:T(8,128)}), f32[1408,256]{1,0:T(8,128)}) %reduce-scatter.38.cloned.1.call-update) | async-done | bytes 1441808 | tf_op jit(solution)/shard_map/reduce_scatter | solution.py:282
  (302 shorter events, 188.7 us)
Async XLA Ops:
  7.2 54.0 %all-gather.35.cloned.1.call-start = ((), (), s32[]{:S(2)}) async-start(), calls=%async_computation.28 | async-start | bytes 1310720 | tf_op jit(solution)/shard_map/all_gather | solution.py:69
  21.2 57.7 %all-gather.37.cloned.1.call-start = ((), (), s32[]{:S(2)}) async-start(), calls=%async_computation.29 | async-start | bytes 2359296 | tf_op jit(solution)/shard_map/all_gather | solution.py:151
  21.9 86.8 %all-gather.23.cloned.1.call-start = ((), (), s32[]{:S(2)}) async-start(), calls=%async_computation.20 | async-start | bytes 2359296 | tf_op jit(solution)/shard_map/all_gather | solution.py:151
  22.7 116.0 %all-gather.21.cloned.1.call-start = ((), (), s32[]{:S(2)}) async-start(), calls=%async_computation.19 | async-start | bytes 1310720 | tf_op jit(solution)/shard_map/all_gather | solution.py:69
  35.2 143.1 %all-gather.39.cloned.1.call-start = ((), (), s32[]{:S(2)}) async-start(), calls=%async_computation.30 | async-start | bytes 2359296 | tf_op jit(solution)/shard_map/all_gather | solution.py:154
  56.1 55.6 %copy-start.13 = (bf16[2048,64]{0,1:T(8,128)(2,1)}, bf16[2048,64]{0,1:T(8,128)(2,1)S(1)}, u32[]{:S(2)}) copy-start(bf16[2048,64]{0,1:T(8,128)(2,1)S(1)} %all_gather.93) | copy-start | bytes 786436
  144.9 13.1 all-to-all-start.2
  148.3 77.7 %reduce-scatter.18.cloned.1.call-start = ((), (), s32[]{:S(2)}) async-start(), calls=%async_computation.31 | async-start | bytes 2621440 | tf_op jit(solution)/shard_map/reduce_scatter | solution.py:73
  177.8 48.2 %copy-start.2 = (bf16[1,64,2048]{2,1,0:T(8,128)(2,1)S(1)}, bf16[1,64,2048]{2,1,0:T(8,128)(2,1)}, u32[]{:S(2)}) copy-start(bf16[1,64,2048]{2,1,0:T(8,128)(2,1)} %param.13) | copy-start | bytes 786436
  178.2 50.8 %copy-start.10 = (bf16[1,256,4,128]{1,3,2,0:T(8,128)(2,1)}, bf16[1,256,4,128]{1,3,2,0:T(8,128)(2,1)S(1)}, u32[]{:S(2)}) copy-start(bf16[1,256,4,128]{1,3,2,0:T(8,128)(2,1)S(1)} %copy.90) | copy-start | bytes 786436
  178.3 53.6 %copy-start.20 = (bf16[1,64,2048]{2,1,0:T(8,128)(2,1)S(1)}, bf16[1,64,2048]{2,1,0:T(8,128)(2,1)}, u32[]{:S(2)}) copy-start(bf16[1,64,2048]{2,1,0:T(8,128)(2,1)} %param.25) | copy-start | bytes 786436
  182.0 74.5 %all-gather.45.cloned.1.call-start = ((), (), s32[]{:S(2)}) async-start(), calls=%async_computation.34 | async-start | bytes 1310720 | tf_op jit(solution)/shard_map/all_gather | solution.py:69
  229.1 72.3 %all-gather.47.cloned.1.call-start = ((), (), s32[]{:S(2)}) async-start(), calls=%async_computation.35 | async-start | bytes 6488064 | tf_op jit(solution)/shard_map/all_gather | solution.py:190
  229.8 116.9 %all-gather.49.cloned.1.call-start = ((), (), s32[]{:S(2)}) async-start(), calls=%async_computation.36 | async-start | bytes 6488064 | tf_op jit(solution)/shard_map/all_gather | solution.py:189
  230.6 146.2 %all-gather.41.cloned.1.call-start = ((), (), s32[]{:S(2)}) async-start(), calls=%async_computation.32 | async-start | bytes 1310720 | tf_op jit(solution)/shard_map/all_gather | solution.py:69
  232.7 190.1 %all-gather.43.cloned.1.call-start = ((), (), s32[]{:S(2)}) async-start(), calls=%async_computation.33 | async-start | bytes 6488064 | tf_op jit(solution)/shard_map/all_gather | solution.py:191
  233.4 247.2 %reduce-scatter.20.cloned.1.call-start = ((), (), s32[]{:S(2)}) async-start(), calls=%async_computation.37 | async-start | bytes 2621440 | tf_op jit(solution)/shard_map/reduce_scatter | solution.py:73
  256.5 90.3 %copy-start.6 = (bf16[1,256,2048]{2,1,0:T(8,128)(2,1)S(1)}, bf16[1,256,2048]{2,1,0:T(8,128)(2,1)}, u32[]{:S(2)}) copy-start(bf16[1,256,2048]{2,1,0:T(8,128)(2,1)} %all-gather.45.cloned.1.call-done) | copy-start | bytes 3145732
  430.7 49.9 %copy-start.4 = (f32[1,64,2048]{2,1,0:T(8,128)S(1)}, f32[1,64,2048]{2,1,0:T(8,128)}, u32[]{:S(2)}) copy-start(f32[1,64,2048]{2,1,0:T(8,128)} %reduce-scatter.18.cloned.1.call-done) | copy-start | bytes 1572868
  430.7 49.9 %copy-start.46 = (f32[64]{0:T(128)S(1)}, f32[64]{0:T(128)}, u32[]{:S(2)}) copy-start(f32[64]{0:T(128)} %copy-done.45) | copy-start | bytes 772
  430.7 51.7 %copy-start.43 = (f32[64]{0:T(128)S(1)}, f32[64]{0:T(128)}, u32[]{:S(2)}) copy-start(f32[64]{0:T(128)} %copy-done.42) | copy-start | bytes 772
  436.6 75.5 %all-gather.51.cloned.1.call-start = ((), (), s32[]{:S(2)}) async-start(), calls=%async_computation.38 | async-start | bytes 1310720 | tf_op jit(solution)/shard_map/all_gather | solution.py:69
  482.5 39.3 %copy-start.39 = (f32[2,1024]{1,0:T(2,128)S(1)}, f32[2,1024]{1,0:T(2,128)}, u32[]{:S(2)}) copy-start(f32[2,1024]{1,0:T(2,128)} %copy-done.38) | copy-start | bytes 24580
  518.2 9.4 all-to-all-start.4
  521.6 63.9 %reduce-scatter.22.cloned.1.call-start = ((), (), s32[]{:S(2)}) async-start(), calls=%async_computation.39 | async-start | bytes 655360 | tf_op jit(solution)/shard_map/reduce_scatter | solution.py:313
  547.0 69.7 %all-gather.25.cloned.1.call-start = ((), (), s32[]{:S(2)}) async-start(), calls=%async_computation.21 | async-start | bytes 2359296 | tf_op jit(solution)/shard_map/all_gather | solution.py:154
  572.6 12.2 all-to-all-start
  576.0 87.6 %reduce-scatter.14.cloned.1.call-start = ((), (), s32[]{:S(2)}) async-start(), calls=%async_computation.22 | async-start | bytes 2621440 | tf_op jit(solution)/shard_map/reduce_scatter | solution.py:73
  620.5 47.6 %copy-start.36 = (f32[1024]{0:T(1024)S(1)}, f32[1024]{0:T(1024)}, u32[]{:S(2)}) copy-start(f32[1024]{0:T(1024)} %copy-done.35) | copy-start | bytes 12292
  620.5 47.6 %copy-start.48 = (f32[32]{0:T(128)S(1)}, f32[32]{0:T(128)}, u32[]{:S(2)}) copy-start(f32[32]{0:T(128)} %copy-done.47) | copy-start | bytes 388
  620.5 87.5 %all-gather.29.cloned.1.call-start = ((), (), s32[]{:S(2)}) async-start(), calls=%async_computation.24 | async-start | bytes 6488064 | tf_op jit(solution)/shard_map/all_gather | solution.py:189
  621.1 116.9 %all-gather.27.cloned.1.call-start = ((), (), s32[]{:S(2)}) async-start(), calls=%async_computation.23 | async-start | bytes 1310720 | tf_op jit(solution)/shard_map/all_gather | solution.py:69
  666.7 116.0 %all-gather.31.cloned.1.call-start = ((), (), s32[]{:S(2)}) async-start(), calls=%async_computation.25 | async-start | bytes 6488064 | tf_op jit(solution)/shard_map/all_gather | solution.py:190
  667.5 161.3 %all-gather.33.cloned.1.call-start = ((), (), s32[]{:S(2)}) async-start(), calls=%async_computation.26 | async-start | bytes 6488064 | tf_op jit(solution)/shard_map/all_gather | solution.py:191
  668.1 206.9 %reduce-scatter.24.cloned.1.call-start = ((), (), s32[]{:S(2)}) async-start(), calls=%async_computation.40 | async-start | bytes 2621440 | tf_op jit(solution)/shard_map/reduce_scatter | solution.py:73
  700.5 220.3 %reduce-scatter.16.cloned.1.call-start = ((), (), s32[]{:S(2)}) async-start(), calls=%async_computation.27 | async-start | bytes 2621440 | tf_op jit(solution)/shard_map/reduce_scatter | solution.py:73
  738.0 90.8 %copy-start.50 = (bf16[1,256,2048]{2,1,0:T(8,128)(2,1)S(1)}, bf16[1,256,2048]{2,1,0:T(8,128)(2,1)}, u32[]{:S(2)}) copy-start(bf16[1,256,2048]{2,1,0:T(8,128)(2,1)} %all-gather.27.cloned.1.call-done) | copy-start | bytes 3145732
  743.9 94.5 %copy-start.28 = (bf16[256,32]{0,1:T(8,128)(2,1)S(1)}, bf16[256,32]{0,1:T(8,128)(2,1)}, u32[]{:S(2)}) copy-start(bf16[256,32]{0,1:T(8,128)(2,1)} %get-tuple-element.116) | copy-start | bytes 49156
  838.3 119.7 %reduce-scatter.28.cloned.1.call-start = ((), (), s32[]{:S(2)}) async-start(), calls=%async_computation.42 | async-start | bytes 589824 | tf_op jit(solution)/shard_map/reduce_scatter | solution.py:339
  839.5 156.5 %reduce-scatter.30.cloned.1.call-start = ((), (), s32[]{:S(2)}) async-start(), calls=%async_computation.43 | async-start | bytes 589824 | tf_op jit(solution)/shard_map/reduce_scatter | solution.py:340
  840.7 210.6 %reduce-scatter.32.cloned.1.call-start = ((), (), s32[]{:S(2)}) async-start(), calls=%async_computation.44 | async-start | bytes 4718592 | tf_op jit(solution)/shard_map/reduce_scatter | solution.py:341
  843.5 263.3 %reduce-scatter.26.cloned.1.call-start = ((), (), s32[]{:S(2)}) async-start(), calls=%async_computation.41 | async-start | bytes 4718592 | tf_op jit(solution)/shard_map/reduce_scatter | solution.py:338
  846.3 351.3 %reduce-scatter.34.cloned.1.call-start = ((), (), s32[]{:S(2)}) async-start(), calls=%async_computation.45 | async-start | bytes 12976128 | tf_op jit(solution)/shard_map/reduce_scatter | solution.py:280
  853.8 434.6 %reduce-scatter.36.cloned.1.call-start = ((), (), s32[]{:S(2)}) async-start(), calls=%async_computation.46 | async-start | bytes 12976128 | tf_op jit(solution)/shard_map/reduce_scatter | solution.py:281
  861.0 518.3 %reduce-scatter.38.cloned.1.call-start = ((), (), s32[]{:S(2)}) async-start(), calls=%async_computation.47 | async-start | bytes 12976128 | tf_op jit(solution)/shard_map/reduce_scatter | solution.py:282
  869.9 41.9 %copy-start.17 = (f32[1,64,2048]{2,1,0:T(8,128)S(1)}, f32[1,64,2048]{2,1,0:T(8,128)}, u32[]{:S(2)}) copy-start(f32[1,64,2048]{2,1,0:T(8,128)} %get-tuple-element.106) | copy-start | bytes 1572868
  869.9 50.9 %copy-start.8 = (f32[1,64,2048]{2,1,0:T(8,128)S(1)}, f32[1,64,2048]{2,1,0:T(8,128)}, u32[]{:S(2)}) copy-start(f32[1,64,2048]{2,1,0:T(8,128)} %reduce-scatter.14.cloned.1.call-done) | copy-start | bytes 1572868
  870.0 50.9 %copy-start.44 = (f32[64]{0:T(128)S(1)}, f32[64]{0:T(128)}, u32[]{:S(2)}) copy-start(f32[64]{0:T(128)} %copy-done.42) | copy-start | bytes 772
  (38 other events, 349.6 us)
Sparse Core Ops, SparseCore 0:
  21.3 28.2 all-gather.34
  51.5 27.3 all-gather.36
  80.8 27.8 all-gather.22
  110.7 27.9 all-gather.20
  140.4 30.5 all-gather.38
  182.2 43.7 reduce-scatter.17
  229.2 27.2 all-gather.44
  258.5 42.7 all-gather.46
  303.4 43.3 all-gather.48
  348.8 27.9 all-gather.40
  378.9 43.8 all-gather.42
  436.7 43.8 reduce-scatter.19
  484.8 27.2 all-gather.50
  547.2 20.9 reduce-scatter.21
  570.0 29.6 all-gather.24
  620.6 42.9 reduce-scatter.13
  665.3 42.6 all-gather.28
  710.0 27.9 all-gather.26
  739.8 42.8 all-gather.30
  784.4 44.3 all-gather.32
  831.1 43.8 reduce-scatter.23
  877.4 43.4 reduce-scatter.15
  924.5 33.4 reduce-scatter.27
  961.8 34.1 reduce-scatter.29
  999.9 51.3 reduce-scatter.31
  1055.4 51.3 reduce-scatter.25
  1110.7 86.7 reduce-scatter.33
  1201.6 86.7 reduce-scatter.35
  1292.5 86.7 reduce-scatter.37
where the time goes:
time: 1400 us; the launch traced here: 1390 us
  waiting for transfers between devices  987 us (70%)
  blocking collectives  157 us (11%)
  matrix products  124 us (9%)
  other arithmetic  52.9 us (4%)
  local copies, waits for them, and re-layouts  37.4 us (3%)
  between operations  16.3 us (1%)
    all_gather x6, waiting for transfers between devices, rows_gather(): return lax.all_gather(activations, 'tensor', axis=1, tiled=True)  128 us
    reduce_scatter x5, waiting for transfers between devices, rows_sum(): return lax.psum_scatter(partials, 'tensor', scatter_dimension=1, tiled=True)  122 us
    all_gather x2, waiting for transfers between devices, forward_pass(): lax.all_gather(w_down, ('fsdp', 'context'), axis=1, tiled=True)  92 us
    reduce_scatter x1, waiting for transfers between devices, body(): lax.psum_scatter(grad_down, ('fsdp', 'context'), scatter_dimension=1, til...  90.9 us
    reduce_scatter x1, waiting for transfers between devices, body(): lax.psum_scatter(grad_up, ('fsdp', 'context'), scatter_dimension=0, tiled...  90.9 us
    reduce_scatter x1, waiting for transfers between devices, body(): lax.psum_scatter(grad_gate, ('fsdp', 'context'), scatter_dimension=0, til...  90.7 us
    all_gather x2, waiting for transfers between devices, forward_pass(): lax.all_gather(w_up, ('fsdp', 'context'), axis=0, tiled=True)  83.7 us
    reduce_scatter x1, waiting for transfers between devices, body(): lax.psum_scatter(grad_query, ('fsdp', 'context'), scatter_dimension=0, ti...  55.5 us
  transfers between devices with their start and end apart: 32, of which 27 were waited for; matrix products, arithmetic and copies ran while one was open for 11% of the time, Pallas kernels for 0%

commit v1 on v0

--- a/solution.py
+++ b/solution.py
@@ -186,7 +186,12 @@
     middle = hidden_f + branch_one
     gain_two, gate_all, up_all, down_all = (
         lax.all_gather(mlp_gain, ("fsdp", "context"), axis=0, tiled=True),
-        lax.all_gather(w_gate, ("fsdp", "context"), axis=0, tiled=True),
+        jnp.concatenate(
+            lax.all_to_all(
+                jnp.stack([w_gate] * lax.axis_size(("fsdp", "context"))), ("fsdp", "context"), 0, 0
+            ),
+            axis=0,
+        ),
         lax.all_gather(w_up, ("fsdp", "context"), axis=0, tiled=True),
         lax.all_gather(w_down, ("fsdp", "context"), axis=1, tiled=True),
     )

time: 1400 us -> 1370 us (0.979)
  waiting for transfers between devices: 987 us -> 869 us
  blocking collectives: 157 us -> 243 us
    all_to_all x0 -> x1, blocking collectives: none -> 88.5 us  [forward_pass(): lax.all_to_all(jnp.stack([w_gate] * lax.axis_size(('fsdp', 'context'))),...]
    all_gather x2, waiting for transfers between devices: 83.7 us -> 0.6 us  [forward_pass(): lax.all_gather(w_up, ('fsdp', 'context'), axis=0, tiled=True)]
    all_to_all x0 -> x1, waiting for transfers between devices: none -> 72.6 us  [forward_pass(): lax.all_to_all(jnp.stack([w_gate] * lax.axis_size(('fsdp', 'context'))),...]
    all_gather x6, waiting for transfers between devices: 128 us -> 74.1 us  [rows_gather(): return lax.all_gather(activations, 'tensor', axis=1, tiled=True)]
    all_gather x2 -> x0, waiting for transfers between devices: 46.7 us -> none  [forward_pass(): lax.all_gather(w_gate, ('fsdp', 'context'), axis=0, tiled=True)]
  transfers between devices with their start and end apart: 32 -> 31, of which waited for: 27 -> 23; matrix products, arithmetic and copies ran while one was open for 11% -> 11% of each run, Pallas kernels for 0% -> 0%
where the time goes in v1:
time: 1370 us; the launch traced here: 1360 us
  waiting for transfers between devices  869 us (63%)
  blocking collectives  243 us (18%)
  matrix products  122 us (9%)
  other arithmetic  54.4 us (4%)
  local copies, waits for them, and re-layouts  41.9 us (3%)
  starting transfers between devices  17.2 us (1%)
  between operations  16.6 us (1%)
    reduce_scatter x5, waiting for transfers between devices, rows_sum(): return lax.psum_scatter(partials, 'tensor', scatter_dimension=1, tiled=True)  123 us
    reduce_scatter x1, waiting for transfers between devices, body(): lax.psum_scatter(grad_gate, ('fsdp', 'context'), scatter_dimension=0, til...  90.9 us
    reduce_scatter x1, waiting for transfers between devices, body(): lax.psum_scatter(grad_up, ('fsdp', 'context'), scatter_dimension=0, tiled...  90.8 us
    reduce_scatter x1, waiting for transfers between devices, body(): lax.psum_scatter(grad_down, ('fsdp', 'context'), scatter_dimension=1, til...  90.7 us
    all_gather x2, waiting for transfers between devices, forward_pass(): lax.all_gather(w_down, ('fsdp', 'context'), axis=1, tiled=True)  90.3 us
    all_to_all x1, blocking collectives, forward_pass(): lax.all_to_all(jnp.stack([w_gate] * lax.axis_size(('fsdp', 'context'))),...  88.5 us
    all_gather x6, waiting for transfers between devices, rows_gather(): return lax.all_gather(activations, 'tensor', axis=1, tiled=True)  74.1 us
    all_to_all x1, waiting for transfers between devices, forward_pass(): lax.all_to_all(jnp.stack([w_gate] * lax.axis_size(('fsdp', 'context'))),...  72.6 us
  transfers between devices with their start and end apart: 31, of which 23 were waited for; matrix products, arithmetic and copies ran while one was open for 11% of the time, Pallas kernels for 0%

profile of v1, /device:TPU:0, one launch (start us, length us, event | category | flops | bytes accessed | tf_op | source)
XLA Modules:
  0.0 1363.5 jit_solution(2128248051814312857)
XLA Ops:
  9.0 10.3 all-gather.2
  23.4 8.8 all-gather
  37.4 9.1 all_gather.85
  46.5 9.6 all_gather.86
  65.9 13.0 all-gather.33.cloned.1.call-done
  83.0 25.7 %all-gather.21.cloned.1.call-done = bf16[2048,512]{1,0:T(8,128)(2,1)} async-done(((bf16[256,512]{1,0:T(8,128)(2,1)}), bf16[2048,512]{1,0:T(8,128)(2,1)}) %all-gather.21.cloned.1.call-update) | async-done | bytes 2097168 | tf_op jit(solution)/shard_map/all_gather | solution.py:151
  114.8 23.8 %all-gather.19.cloned.1.call-done = bf16[1,256,2048]{2,1,0:T(8,128)(2,1)} async-done(((bf16[1,64,2048]{2,1,0:T(8,128)(2,1)}), bf16[1,256,2048]{2,1,0:T(8,128)(2,1)}) %all-gather.19.cloned.1.call-update) | async-done | bytes 1048592 | tf_op jit(solution)/shard_map/all_gather | solution.py:69
  149.1 8.9 all_gather.87
  168.1 8.4 all_to_all.100
  180.9 9.0 all-gather.3
  189.9 35.0 %reduce-scatter.18.cloned.1.call-done = f32[1,64,2048]{2,1,0:T(8,128)} async-done(((f32[1,256,2048]{2,1,0:T(8,128)}), f32[1,64,2048]{2,1,0:T(8,128)}) %reduce-scatter.18.cloned.1.call-update) | async-done | bytes 524304 | tf_op jit(solution)/shard_map/reduce_scatter | solution.py:73
  231.4 88.5 %all_to_all.101 = bf16[8,256,1408]{2,1,0:T(8,128)(2,1)} all-to-all(bf16[8,256,1408]{2,1,0:T(8,128)(2,1)S(1)} %stack.5), channel_id=1, replica_groups=mesh['fsdp'=2,'context'=4,'tensor'=4] {'fsdp','context'}, dimensions={0} | all-to-all | bytes 11534336 | tf_op jit(solution)/shard_map/all_to_all | solution.py:190
  319.9 6.0 fusion.38
  325.9 5.6 fusion.40
  331.5 22.8 %all-gather.37.cloned.1.call-done = bf16[1,256,2048]{2,1,0:T(8,128)(2,1)} async-done(((bf16[1,64,2048]{2,1,0:T(8,128)(2,1)}), bf16[1,256,2048]{2,1,0:T(8,128)(2,1)}) %all-gather.37.cloned.1.call-update) | async-done | bytes 1048592 | tf_op jit(solution)/shard_map/all_gather | solution.py:69
  354.3 45.8 %all-gather.39.cloned.1.call-done = bf16[1408,2048]{1,0:T(8,128)(2,1)} async-done(((bf16[1408,256]{1,0:T(8,128)(2,1)}), bf16[1408,2048]{1,0:T(8,128)(2,1)}) %all-gather.39.cloned.1.call-update) | async-done | bytes 5767184 | tf_op jit(solution)/shard_map/all_gather | solution.py:196
  400.1 6.1 multiply_convert_fusion.1
  412.6 44.0 %reduce-scatter.20.cloned.1.call-done = f32[1,64,2048]{2,1,0:T(8,128)} async-done(((f32[1,256,2048]{2,1,0:T(8,128)}), f32[1,64,2048]{2,1,0:T(8,128)}) %reduce-scatter.20.cloned.1.call-update) | async-done | bytes 524304 | tf_op jit(solution)/shard_map/reduce_scatter | solution.py:73
  460.6 27.4 %all-gather.45.cloned.1.call-done = bf16[1,256,2048]{2,1,0:T(8,128)(2,1)} async-done(((bf16[1,64,2048]{2,1,0:T(8,128)(2,1)}), bf16[1,256,2048]{2,1,0:T(8,128)(2,1)}) %all-gather.45.cloned.1.call-update) | async-done | bytes 1048592 | tf_op jit(solution)/shard_map/all_gather | solution.py:69
  497.7 5.8 all-to-all-done.6
  504.2 5.1 fusion.1
  509.3 4.8 fusion.24
  523.6 10.8 all_gather.74
  534.3 9.9 all_gather.75
  566.9 7.6 all_gather.76
  574.5 6.5 fusion.117
  587.9 8.4 all_to_all.102
  600.6 8.9 all-gather.1
  609.5 34.3 %reduce-scatter.14.cloned.1.call-done = f32[1,64,2048]{2,1,0:T(8,128)} async-done(((f32[1,256,2048]{2,1,0:T(8,128)}), f32[1,64,2048]{2,1,0:T(8,128)}) %reduce-scatter.14.cloned.1.call-update) | async-done | bytes 524304 | tf_op jit(solution)/shard_map/reduce_scatter | solution.py:73
  654.5 9.1 all_to_all.103
  666.5 4.8 all-to-all-start.2
  682.0 72.6 %all-to-all-done.2 = bf16[8,256,1408]{2,1,0:T(8,128)(2,1)} async-done(((bf16[8,256,1408]{2,1,0:T(8,128)(2,1)}), bf16[8,256,1408]{2,1,0:T(8,128)(2,1)}, u32[]{:S(2)}, u32[]{:S(2)}) %all-to-all-start.2) | async-done | bytes 5767200 | tf_op jit(solution)/shard_map/all_to_all | solution.py:190
  754.7 6.0 fusion.56
  761.3 44.6 %all-gather.29.cloned.1.call-done = bf16[1408,2048]{1,0:T(8,128)(2,1)} async-done(((bf16[1408,256]{1,0:T(8,128)(2,1)}), bf16[1408,2048]{1,0:T(8,128)(2,1)}) %all-gather.29.cloned.1.call-update) | async-done | bytes 5767184 | tf_op jit(solution)/shard_map/all_gather | solution.py:196
  805.9 9.5 convolution_bitcast_fusion.1
  824.8 6.1 fusion.36
  832.0 6.1 fusion.34
  839.7 7.3 fusion.42
  853.4 23.9 %all-reduce.2 = (f32[2048]{0:T(1024)S(1)}, f32[2048]{0:T(1024)S(1)}) all-reduce(f32[2048]{0:T(1024)S(1)} %get-tuple-element.99, f32[2048]{0:T(1024)S(1)} %copy-done.45), channel_id=8, replica_groups=mesh['fsdp'=2,'context'=4,'tensor'=4] {'fsdp','context'}, use_global_device_ids=true, to_apply=%region_21.22.clone | all-reduce | flops 4096 | bytes 32768
  877.5 11.4 all-reduce.3
  890.9 6.8 reduce-scatter.16.cloned.1.call-done
  899.6 35.3 %reduce-scatter.28.cloned.1.call-done = f32[256,64]{0,1:T(8,128)} async-done(((f32[2048,64]{0,1:T(8,128)}), f32[256,64]{0,1:T(8,128)}) %reduce-scatter.28.cloned.1.call-update) | async-done | bytes 65552 | tf_op jit(solution)/shard_map/reduce_scatter | solution.py:344
  934.9 38.1 %reduce-scatter.30.cloned.1.call-done = f32[256,64]{0,1:T(8,128)} async-done(((f32[2048,64]{0,1:T(8,128)}), f32[256,64]{0,1:T(8,128)}) %reduce-scatter.30.cloned.1.call-update) | async-done | bytes 65552 | tf_op jit(solution)/shard_map/reduce_scatter | solution.py:345
  973.0 55.3 %reduce-scatter.32.cloned.1.call-done = f32[512,256]{1,0:T(8,128)} async-done(((f32[512,2048]{1,0:T(8,128)}), f32[512,256]{1,0:T(8,128)}) %reduce-scatter.32.cloned.1.call-update) | async-done | bytes 524304 | tf_op jit(solution)/shard_map/reduce_scatter | solution.py:346
  1028.3 55.5 %reduce-scatter.26.cloned.1.call-done = f32[256,512]{1,0:T(8,128)} async-done(((f32[2048,512]{1,0:T(8,128)}), f32[256,512]{1,0:T(8,128)}) %reduce-scatter.26.cloned.1.call-update) | async-done | bytes 524304 | tf_op jit(solution)/shard_map/reduce_scatter | solution.py:343
  1083.8 90.9 %reduce-scatter.34.cloned.1.call-done = f32[256,1408]{1,0:T(8,128)} async-done(((f32[2048,1408]{1,0:T(8,128)}), f32[256,1408]{1,0:T(8,128)}) %reduce-scatter.34.cloned.1.call-update) | async-done | bytes 1441808 | tf_op jit(solution)/shard_map/reduce_scatter | solution.py:285
  1174.7 90.8 %reduce-scatter.36.cloned.1.call-done = f32[256,1408]{1,0:T(8,128)} async-done(((f32[2048,1408]{1,0:T(8,128)}), f32[256,1408]{1,0:T(8,128)}) %reduce-scatter.36.cloned.1.call-update) | async-done | bytes 1441808 | tf_op jit(solution)/shard_map/reduce_scatter | solution.py:286
  1265.5 90.7 %reduce-scatter.38.cloned.1.call-done = f32[1408,256]{1,0:T(8,128)} async-done(((f32[1408,2048]{1,0:T(8,128)}), f32[1408,256]{1,0:T(8,128)}) %reduce-scatter.38.cloned.1.call-update) | async-done | bytes 1441808 | tf_op jit(solution)/shard_map/reduce_scatter | solution.py:287
  (307 shorter events, 172.1 us)
Async XLA Ops:
  7.2 54.0 %all-gather.31.cloned.1.call-start = ((), (), s32[]{:S(2)}) async-start(), calls=%async_computation.29 | async-start | bytes 1310720 | tf_op jit(solution)/shard_map/all_gather | solution.py:69
  21.2 57.7 %all-gather.33.cloned.1.call-start = ((), (), s32[]{:S(2)}) async-start(), calls=%async_computation.30 | async-start | bytes 2359296 | tf_op jit(solution)/shard_map/all_gather | solution.py:151
  21.9 86.8 %all-gather.21.cloned.1.call-start = ((), (), s32[]{:S(2)}) async-start(), calls=%async_computation.22 | async-start | bytes 2359296 | tf_op jit(solution)/shard_map/all_gather | solution.py:151
  22.7 116.0 %all-gather.19.cloned.1.call-start = ((), (), s32[]{:S(2)}) async-start(), calls=%async_computation.21 | async-start | bytes 1310720 | tf_op jit(solution)/shard_map/all_gather | solution.py:69
  35.2 141.9 %all-gather.35.cloned.1.call-start = ((), (), s32[]{:S(2)}) async-start(), calls=%async_computation.31 | async-start | bytes 2359296 | tf_op jit(solution)/shard_map/all_gather | solution.py:154
  56.1 55.6 %copy-start.15 = (bf16[2048,64]{0,1:T(8,128)(2,1)}, bf16[2048,64]{0,1:T(8,128)(2,1)S(1)}, u32[]{:S(2)}) copy-start(bf16[2048,64]{0,1:T(8,128)(2,1)S(1)} %all_gather.86) | copy-start | bytes 786436
  78.9 32.8 %copy-start.3 = (bf16[1,256,2048]{2,1,0:T(8,128)(2,1)S(1)}, bf16[1,256,2048]{2,1,0:T(8,128)(2,1)}, u32[]{:S(2)}) copy-start(bf16[1,256,2048]{2,1,0:T(8,128)(2,1)} %all-gather.31.cloned.1.call-done) | copy-start | bytes 3145732
  145.6 12.4 all-to-all-start.3
  149.0 75.8 %reduce-scatter.18.cloned.1.call-start = ((), (), s32[]{:S(2)}) async-start(), calls=%async_computation.32 | async-start | bytes 2621440 | tf_op jit(solution)/shard_map/reduce_scatter | solution.py:73
  176.5 48.3 %copy-start.2 = (bf16[1,64,2048]{2,1,0:T(8,128)(2,1)S(1)}, bf16[1,64,2048]{2,1,0:T(8,128)(2,1)}, u32[]{:S(2)}) copy-start(bf16[1,64,2048]{2,1,0:T(8,128)(2,1)} %param.13) | copy-start | bytes 786436
  177.0 50.9 %copy-start.11 = (bf16[1,256,4,128]{1,3,2,0:T(8,128)(2,1)}, bf16[1,256,4,128]{1,3,2,0:T(8,128)(2,1)S(1)}, u32[]{:S(2)}) copy-start(bf16[1,256,4,128]{1,3,2,0:T(8,128)(2,1)S(1)} %copy.90) | copy-start | bytes 786436
  177.1 52.4 %copy-start.22 = (bf16[1,64,2048]{2,1,0:T(8,128)(2,1)S(1)}, bf16[1,64,2048]{2,1,0:T(8,128)(2,1)}, u32[]{:S(2)}) copy-start(bf16[1,64,2048]{2,1,0:T(8,128)(2,1)} %param.25) | copy-start | bytes 786436
  180.8 50.2 %copy-start.13 = (bf16[256,1408]{1,0:T(8,128)(2,1)S(1)}, bf16[256,1408]{1,0:T(8,128)(2,1)}, u32[]{:S(2)}) copy-start(bf16[256,1408]{1,0:T(8,128)(2,1)} %param.22) | copy-start | bytes 2162692
  180.8 139.1 %all-gather.41.cloned.1.call-start = ((), (), s32[]{:S(2)}) async-start(), calls=%async_computation.35 | async-start | bytes 1310720 | tf_op jit(solution)/shard_map/all_gather | solution.py:69
  227.9 98.0 %all-gather.43.cloned.1.call-start = ((), (), s32[]{:S(2)}) async-start(), calls=%async_computation.36 | async-start | bytes 6488064 | tf_op jit(solution)/shard_map/all_gather | solution.py:195
  228.7 125.6 %all-gather.37.cloned.1.call-start = ((), (), s32[]{:S(2)}) async-start(), calls=%async_computation.33 | async-start | bytes 1310720 | tf_op jit(solution)/shard_map/all_gather | solution.py:69
  229.5 228.9 %copy-start.48 = (f32[64]{0:T(128)}, f32[64]{0:T(128)S(1)}, u32[]{:S(2)}) copy-start(f32[64]{0:T(128)S(1)} %convert_bitcast_fusion) | copy-start | bytes 772
  230.3 169.8 %all-gather.39.cloned.1.call-start = ((), (), s32[]{:S(2)}) async-start(), calls=%async_computation.34 | async-start | bytes 6488064 | tf_op jit(solution)/shard_map/all_gather | solution.py:196
  230.9 225.6 %reduce-scatter.20.cloned.1.call-start = ((), (), s32[]{:S(2)}) async-start(), calls=%async_computation.37 | async-start | bytes 2621440 | tf_op jit(solution)/shard_map/reduce_scatter | solution.py:73
  409.4 47.2 %copy-start.4 = (f32[1,64,2048]{2,1,0:T(8,128)S(1)}, f32[1,64,2048]{2,1,0:T(8,128)}, u32[]{:S(2)}) copy-start(f32[1,64,2048]{2,1,0:T(8,128)} %reduce-scatter.18.cloned.1.call-done) | copy-start | bytes 1572868
  409.4 49.0 %copy-start.23 = (bf16[1,64,2048]{2,1,0:T(8,128)(2,1)S(1)}, bf16[1,64,2048]{2,1,0:T(8,128)(2,1)}, u32[]{:S(2)}) copy-start(bf16[1,64,2048]{2,1,0:T(8,128)(2,1)} %param.25) | copy-start | bytes 786436
  412.5 75.4 %all-gather.45.cloned.1.call-start = ((), (), s32[]{:S(2)}) async-start(), calls=%async_computation.38 | async-start | bytes 1310720 | tf_op jit(solution)/shard_map/all_gather | solution.py:69
  494.1 9.4 all-to-all-start.6
  497.5 66.3 %reduce-scatter.22.cloned.1.call-start = ((), (), s32[]{:S(2)}) async-start(), calls=%async_computation.39 | async-start | bytes 655360 | tf_op jit(solution)/shard_map/reduce_scatter | solution.py:318
  520.7 35.3 %copy-start.10 = (bf16[1,256,2048]{2,1,0:T(8,128)(2,1)S(1)}, bf16[1,256,2048]{2,1,0:T(8,128)(2,1)}, u32[]{:S(2)}) copy-start(bf16[1,256,2048]{2,1,0:T(8,128)(2,1)} %all-gather.19.cloned.1.call-done) | copy-start | bytes 3145732
  523.0 73.8 %all-gather.23.cloned.1.call-start = ((), (), s32[]{:S(2)}) async-start(), calls=%async_computation.23 | async-start | bytes 2359296 | tf_op jit(solution)/shard_map/all_gather | solution.py:154
  552.0 10.1 all-to-all-start
  556.0 87.8 %reduce-scatter.14.cloned.1.call-start = ((), (), s32[]{:S(2)}) async-start(), calls=%async_computation.24 | async-start | bytes 2621440 | tf_op jit(solution)/shard_map/reduce_scatter | solution.py:73
  596.8 51.2 %copy-start.44 = (f32[1024]{0:T(1024)S(1)}, f32[1024]{0:T(1024)}, u32[]{:S(2)}) copy-start(f32[1024]{0:T(1024)} %copy-done.43) | copy-start | bytes 12292
  596.8 51.2 %copy-start.51 = (f32[32]{0:T(128)S(1)}, f32[32]{0:T(128)}, u32[]{:S(2)}) copy-start(f32[32]{0:T(128)} %copy-done.50) | copy-start | bytes 388
  600.5 154.1 %all-gather.25.cloned.1.call-start = ((), (), s32[]{:S(2)}) async-start(), calls=%async_computation.25 | async-start | bytes 1310720 | tf_op jit(solution)/shard_map/all_gather | solution.py:69
  646.9 114.4 %all-gather.27.cloned.1.call-start = ((), (), s32[]{:S(2)}) async-start(), calls=%async_computation.26 | async-start | bytes 6488064 | tf_op jit(solution)/shard_map/all_gather | solution.py:195
  647.5 158.4 %all-gather.29.cloned.1.call-start = ((), (), s32[]{:S(2)}) async-start(), calls=%async_computation.27 | async-start | bytes 6488064 | tf_op jit(solution)/shard_map/all_gather | solution.py:196
  666.5 88.1 %all-to-all-start.2 = ((bf16[8,256,1408]{2,1,0:T(8,128)(2,1)}), bf16[8,256,1408]{2,1,0:T(8,128)(2,1)}, u32[]{:S(2)}, u32[]{:S(2)}) async-start(bf16[8,256,1408]{2,1,0:T(8,128)(2,1)} %stack.4), calls=%async_computation.3 | async-start | bytes 11534336 | tf_op jit(solution)/shard_map/all_to_all | solution.py:190
  671.4 180.7 %reduce-scatter.24.cloned.1.call-start = ((), (), s32[]{:S(2)}) async-start(), calls=%async_computation.40 | async-start | bytes 2621440 | tf_op jit(solution)/shard_map/reduce_scatter | solution.py:73
  681.7 216.0 %reduce-scatter.16.cloned.1.call-start = ((), (), s32[]{:S(2)}) async-start(), calls=%async_computation.28 | async-start | bytes 2621440 | tf_op jit(solution)/shard_map/reduce_scatter | solution.py:73
  754.7 51.2 %copy-start.53 = (bf16[1,256,2048]{2,1,0:T(8,128)(2,1)S(1)}, bf16[1,256,2048]{2,1,0:T(8,128)(2,1)}, u32[]{:S(2)}) copy-start(bf16[1,256,2048]{2,1,0:T(8,128)(2,1)} %all-gather.25.cloned.1.call-done) | copy-start | bytes 3145732
  760.7 54.7 %copy-start.34 = (bf16[256,32]{0,1:T(8,128)(2,1)S(1)}, bf16[256,32]{0,1:T(8,128)(2,1)}, u32[]{:S(2)}) copy-start(bf16[256,32]{0,1:T(8,128)(2,1)} %get-tuple-element.116) | copy-start | bytes 49156
  815.4 119.5 %reduce-scatter.28.cloned.1.call-start = ((), (), s32[]{:S(2)}) async-start(), calls=%async_computation.42 | async-start | bytes 589824 | tf_op jit(solution)/shard_map/reduce_scatter | solution.py:344
  816.6 156.4 %reduce-scatter.30.cloned.1.call-start = ((), (), s32[]{:S(2)}) async-start(), calls=%async_computation.43 | async-start | bytes 589824 | tf_op jit(solution)/shard_map/reduce_scatter | solution.py:345
  817.8 210.5 %reduce-scatter.32.cloned.1.call-start = ((), (), s32[]{:S(2)}) async-start(), calls=%async_computation.44 | async-start | bytes 4718592 | tf_op jit(solution)/shard_map/reduce_scatter | solution.py:346
  820.5 263.3 %reduce-scatter.26.cloned.1.call-start = ((), (), s32[]{:S(2)}) async-start(), calls=%async_computation.41 | async-start | bytes 4718592 | tf_op jit(solution)/shard_map/reduce_scatter | solution.py:343
  823.3 351.4 %reduce-scatter.34.cloned.1.call-start = ((), (), s32[]{:S(2)}) async-start(), calls=%async_computation.45 | async-start | bytes 12976128 | tf_op jit(solution)/shard_map/reduce_scatter | solution.py:285
  830.9 434.6 %reduce-scatter.36.cloned.1.call-start = ((), (), s32[]{:S(2)}) async-start(), calls=%async_computation.46 | async-start | bytes 12976128 | tf_op jit(solution)/shard_map/reduce_scatter | solution.py:286
  838.1 518.1 %reduce-scatter.38.cloned.1.call-start = ((), (), s32[]{:S(2)}) async-start(), calls=%async_computation.47 | async-start | bytes 12976128 | tf_op jit(solution)/shard_map/reduce_scatter | solution.py:287
  847.0 41.9 %copy-start.19 = (f32[1,64,2048]{2,1,0:T(8,128)S(1)}, f32[1,64,2048]{2,1,0:T(8,128)}, u32[]{:S(2)}) copy-start(f32[1,64,2048]{2,1,0:T(8,128)} %get-tuple-element.106) | copy-start | bytes 1572868
  847.0 50.7 %copy-start.9 = (f32[1,64,2048]{2,1,0:T(8,128)S(1)}, f32[1,64,2048]{2,1,0:T(8,128)}, u32[]{:S(2)}) copy-start(f32[1,64,2048]{2,1,0:T(8,128)} %reduce-scatter.14.cloned.1.call-done) | copy-start | bytes 1572868
  847.0 50.7 %copy-start.49 = (f32[64]{0:T(128)S(1)}, f32[64]{0:T(128)}, u32[]{:S(2)}) copy-start(f32[64]{0:T(128)} %copy-done.48) | copy-start | bytes 772
  (40 other events, 316.4 us)
Sparse Core Ops, SparseCore 0:
  21.3 28.2 all-gather.30
  51.5 27.3 all-gather.32
  80.8 27.8 all-gather.20
  110.7 27.9 all-gather.18
  140.4 30.4 all-gather.34
  180.9 43.8 reduce-scatter.17
  228.1 27.2 all-gather.40
  257.4 68.2 all-gather.42
  328.0 26.3 all-gather.36
  356.2 43.8 all-gather.38
  412.6 43.8 reduce-scatter.19
  460.7 27.2 all-gather.44
  523.1 20.3 reduce-scatter.21
  545.4 30.3 all-gather.22
  600.7 43.0 reduce-scatter.13
  647.0 27.2 all-gather.24
  676.0 85.1 all-gather.26
  763.0 42.7 all-gather.28
  808.1 43.8 reduce-scatter.23
  854.3 43.4 reduce-scatter.15
  901.4 33.4 reduce-scatter.27
  938.8 34.1 reduce-scatter.29
  977.0 51.2 reduce-scatter.31
  1032.4 51.3 reduce-scatter.25
  1087.9 86.7 reduce-scatter.33
  1178.7 86.7 reduce-scatter.35
  1269.4 86.7 reduce-scatter.37
